TPU v7x, 32 devices: a whole 2x2x4 slice. The times are simulated.
32 devices in a mesh: depth: 2 (over core), rows: 2 (over x), shots: 8 (over z, y).
Axes of the slice: x: 2, y: 2, z: 4, core: 2. Of those that a mesh axis runs over, the one named last changes fastest.
Arguments:
- sources: float32 [2, 2, 1024, 1024], P('depth', None, 'rows', 'shots'), may hold values from -6 to 6
- factor: float32 [2, 2, 1024, 1024], P('depth', None, ('rows', 'shots')), may hold values from -0.09375 to 0.09375
- block_mask: int32 [2, 2, 8, 8], P('depth'), may hold values 0 or 1
- inverse_diagonal: float32 [2, 2, 1024, 1024], P('depth', None, None, 'rows'), may hold values from -1.2 to 1.2, as said below
Outputs:
- solution: float32 [2, 2, 1024, 1024], P('depth', None, 'rows', 'shots')
Inputs may be any that keep to these rules, and one draw needn't show every extreme that they name: Each block inverse_diagonal[d, m] is lower triangular with diagonal entries between 0.8 and 1.2.
All inputs are finite; a program needn't handle non-finite values. No bound on the sum of `block_mask` on one device may be relied on, other than what follows from the above.
Results may differ from a plain program's by a relative error of at most 0.0001.
Values sent between devices are 32-bit elements; how exact they have to be, the bound alone decides.
No kernel may reach another device: no remote copies, remote signals or barrier semaphores. Data moves between devices by JAX's collectives and lax.ppermute only.
A program may use at most 64 MiB of HBM per device.

v0:
```python
import jax
import jax.numpy as jnp
from jax import lax
from jax.sharding import PartitionSpec as P


def mask_rows(factor_rows, block_mask, row_start, block_size):
    row_total = factor_rows.shape[1]
    block_count = block_mask.shape[3]
    row_blocks = (row_start + jnp.arange(row_total, dtype=jnp.int32)) // block_size
    row_select = (row_blocks[:, None] == jnp.arange(block_count, dtype=jnp.int32)[None, :]).astype(
        jnp.float32
    )
    row_masks = jnp.einsum("rk,pkc->prc", row_select, block_mask[0].astype(jnp.float32))
    return factor_rows * jnp.repeat(row_masks, block_size, axis=2)


def group_reduce(partial_value):
    summed = lax.psum_scatter(partial_value, "depth", scatter_dimension=0, tiled=True)
    return summed[0]


def group_collect(spread):
    every_rows = lax.all_gather(spread[None], "depth", axis=0, tiled=True)
    return every_rows


def invert_level(inverse_block, own_rows):
    inverse_term = jnp.dot(
        inverse_block, own_rows, precision=lax.Precision.HIGHEST, preferred_element_type=jnp.float32
    )
    return lax.psum(inverse_term, "rows")


def per_device(sources, factor, block_mask, inverse_diagonal):
    depth_count = lax.axis_size("depth")
    tree_height = depth_count.bit_length() - 1
    level_count = tree_height + 1
    rows_index = lax.axis_index("rows")
    full_width = factor.shape[3]
    block_count = block_mask.shape[3]
    block_size = full_width // block_count
    highest = lax.Precision.HIGHEST
    front_factor = lax.all_gather(factor[0], "shots", axis=1, tiled=True)
    front_count = front_factor.shape[1]
    masked = mask_rows(front_factor, block_mask, rows_index * front_count, block_size)
    solved = []
    for tier_index in range(level_count):
        own_rows = sources[0, tier_index]
        if tier_index > 0:
            group_size = 2**tier_index
            factor_tiles = masked.reshape(tier_index, group_size, front_count, full_width)
            lower_solved = jnp.stack(solved[:tier_index])
            partial_value = jnp.einsum(
                "lgrs,lsn->grn",
                factor_tiles,
                lower_solved,
                precision=highest,
                preferred_element_type=jnp.float32,
            )
            reduced = group_reduce(partial_value)
            own_rows = own_rows - reduced
        full_rows = invert_level(inverse_diagonal[0, tier_index], own_rows)
        solved.append(full_rows)
    answers = [None] * level_count
    collected = {}
    for tier_index in reversed(range(level_count)):
        target = solved[tier_index]
        if tier_index < tree_height:
            factor_tiles = masked
            transposed = jnp.einsum(
                "grs,grn->sn",
                factor_tiles,
                collected[1],
                precision=highest,
                preferred_element_type=jnp.float32,
            )
            own_columns = lax.psum(transposed, "rows")
            target = target - own_columns
        answer = lax.dot_general(
            inverse_diagonal[0, tier_index],
            target,
            (((0,), (0,)), ((), ())),
            precision=highest,
            preferred_element_type=jnp.float32,
        )
        answers[tier_index] = answer
        if tier_index > 0:
            collected[tier_index] = group_collect(answer)
    return jnp.stack(answers)[None]


def solution(mesh):
    placed = (
        P("depth", None, "rows", "shots"),
        P("depth", None, ("rows", "shots"), None),
        P("depth", None, None, None),
        P("depth", None, None, "rows"),
    )
    return jax.shard_map(
        per_device,
        mesh=mesh,
        in_specs=placed,
        out_specs=P("depth", None, "rows", "shots"),
        check_vma=False,
    )
```

profile of v0, /device:TPU:0, one launch (start us, length us, event | category | flops | bytes accessed | tf_op | source)
XLA Modules:
  0.0 194.4 jit_solution(14296305653696996673)
XLA Ops:
  7.4 0.0 all-reduce.4.cloned.1.call-start
  7.4 4.2 %fusion.6 = f32[1024,128]{1,0:T(8,128)} fusion(f32[1,2,1024,512]{3,2,1,0:T(8,128)} %param.7, f32[1,2,512,128]{3,2,1,0:T(8,128)} %param.4), kind=kOutput, calls=%fused_computation.7 | convolution fusion | flops 805306368 | bytes 2883584 | tf_op jit(solution)/shard_map/dot_general | solution.py:29
  11.5 0.0 all-reduce.4.cloned.1.call-update
  11.6 0.0 all-gather.4.cloned.1.call-start
  11.6 0.5 all-gather.4.cloned.1.call-update
  12.2 0.0 reduce-scatter.2.cloned.1.call-start
  12.2 0.7 convert_bitcast_fusion
  12.9 0.1 copy.5
  13.0 0.1 convolution_bitcast_fusion
  13.1 0.2 copy.6
  13.3 2.6 %broadcast_in_dim.11 = f32[2,512,8,128]{3,2,1,0:T(8,128)} broadcast(f32[2,512,8]{2,1,0:T(8,128)S(1)} %copy.6), dimensions={0,1,2} | broadcast | bytes 4227072 | tf_op jit(solution)/shard_map/broadcast_in_dim | solution.py:15
  15.9 4.9 %reshape.30 = f32[2,512,1024]{2,1,0:T(8,128)} reshape(f32[2,512,8,128]{3,2,1,0:T(8,128)} %broadcast_in_dim.11) | data formatting | bytes 8388608 | tf_op jit(solution)/shard_map/reshape | solution.py:15
  20.8 22.3 %all-reduce.4.cloned.1.call-done = f32[1024,128]{1,0:T(8,128)} async-done(((f32[1024,128]{1,0:T(8,128)}), f32[1024,128]{1,0:T(8,128)}) %all-reduce.4.cloned.1.call-update) | async-done | bytes 524304 | tf_op jit(solution)/shard_map/psum | solution.py:32
  43.1 46.4 %all-gather.4.cloned.1.call-done = f32[1,2,512,1024]{3,2,1,0:T(8,128)} async-done(((f32[1,2,64,1024]{3,2,1,0:T(8,128)}), f32[1,2,512,1024]{3,2,1,0:T(8,128)}) %all-gather.4.cloned.1.call-update) | async-done | bytes 4194320 | tf_op jit(solution)/shard_map/all_gather | solution.py:44
  89.5 7.7 %fusion.13 = f32[2,512,128]{2,1,0:T(8,128)} fusion(f32[2,512,1024]{2,1,0:T(8,128)} %reshape.30, f32[1,2,512,1024]{3,2,1,0:T(8,128)} %all-gather.4.cloned.1.call-done, f32[1024,128]{1,0:T(8,128)} %all-reduce.4.cloned.1.call-done), kind=kOutput, calls=%fused_computation.14 | convolution fusion | flops 1611661312 | bytes 9437184 | tf_op jit(solution)/shard_map/lgrs,lsn->grn/dot_general | solution.py:54
  97.2 0.0 reduce-scatter.2.cloned.1.call-update
  97.3 0.0 all-reduce.6.cloned.1.call-start
  97.3 6.6 %reduce-scatter.2.cloned.1.call-done = f32[1,512,128]{2,1,0:T(8,128)} async-done(((f32[2,512,128]{2,1,0:T(8,128)}), f32[1,512,128]{2,1,0:T(8,128)}) %reduce-scatter.2.cloned.1.call-update) | async-done | bytes 262160 | tf_op jit(solution)/shard_map/reduce_scatter | solution.py:19
  103.9 0.0 copy-done.1
  103.9 4.8 %fusion.15 = f32[1024,128]{0,1:T(8,128)} fusion(f32[1,2,1024,512]{3,2,1,0:T(8,128)} %param.7, f32[1,512,128]{2,1,0:T(8,128)} %reduce-scatter.2.cloned.1.call-done, f32[1,2,512,128]{3,2,1,0:T(8,128)S(1)} %copy-done.1), kind=kOutput, calls=%fused_computation.16 | convolution fusion | flops 805371904 | bytes 3145728 | tf_op jit(solution)/shard_map/dot_general | solution.py:29
  108.7 0.0 all-reduce.6.cloned.1.call-update
  108.7 0.0 all-reduce.8.cloned.1.call-start
  108.8 29.9 %all-reduce.6.cloned.1.call-done = f32[1024,128]{0,1:T(8,128)} async-done(((f32[1024,128]{0,1:T(8,128)}), f32[1024,128]{0,1:T(8,128)}) %all-reduce.6.cloned.1.call-update) | async-done | bytes 524304 | tf_op jit(solution)/shard_map/psum | solution.py:32
  138.7 3.1 %fusion = f32[128,512]{1,0:T(8,128)S(1)} fusion(f32[1024,128]{0,1:T(8,128)} %all-reduce.6.cloned.1.call-done, f32[1,2,1024,512]{3,2,1,0:T(8,128)} %param.7), kind=kOutput, calls=%fused_computation.1 | convolution fusion | flops 805306368 | bytes 2883584 | tf_op jit(solution)/shard_map/dot_general | solution.py:80
  141.7 2.4 %all-gather.1 = f32[1024,128]{0,1:T(8,128)S(1)} all-gather(f32[512,128]{0,1:T(8,128)S(1)} %bitcast.63), channel_id=3, replica_groups=mesh['depth'=2,'rows'=2,'shots'=8] {'depth'}, dimensions={0}, use_global_device_ids=true | all-gather | bytes 786432 | tf_op jit(solution)/shard_map/all_gather | solution.py:24
  144.1 0.2 copy.9
  144.3 0.0 copy-start
  144.3 10.0 %fusion.14 = f32[1024,128]{1,0:T(8,128)} fusion(f32[2,512,128]{2,1,0:T(8,128)S(1)} %bitcast.65, f32[2,512,1024]{2,1,0:T(8,128)} %reshape.30, f32[1,2,512,1024]{3,2,1,0:T(8,128)} %all-gather.4.cloned.1.call-done), kind=kOutput, calls=%fused_computation.15 | convolution fusion | flops 1611661312 | bytes 9437184 | tf_op jit(solution)/shard_map/grs,grn->sn/dot_general | solution.py:71
  154.3 0.0 all-reduce.8.cloned.1.call-update
  154.3 28.8 %all-reduce.8.cloned.1.call-done = f32[1024,128]{1,0:T(8,128)} async-done(((f32[1024,128]{1,0:T(8,128)}), f32[1024,128]{1,0:T(8,128)}) %all-reduce.8.cloned.1.call-update) | async-done | bytes 524304 | tf_op jit(solution)/shard_map/psum | solution.py:78
  183.1 3.2 %fusion.18 = f32[1,512,128]{1,2,0:T(8,128)S(1)} fusion(f32[1,2,1024,512]{3,2,1,0:T(8,128)} %param.7, f32[1024,128]{1,0:T(8,128)S(1)} %copy-done, f32[1024,128]{1,0:T(8,128)} %all-reduce.8.cloned.1.call-done), kind=kOutput, calls=%fused_computation.17 | convolution fusion | flops 805437440 | bytes 3407872 | tf_op jit(solution)/shard_map/dot_general | solution.py:80
  186.3 1.0 copy.7
  (4 shorter events, 0.1 us)
Async XLA Ops:
  7.4 35.7 %all-reduce.4.cloned.1.call-start = ((), (), s32[]{:S(2)}) async-start(), calls=%async_computation.1 | async-start | bytes 1048576 | tf_op jit(solution)/shard_map/psum | solution.py:32
  11.6 78.0 %all-gather.4.cloned.1.call-start = ((), (), s32[]{:S(2)}) async-start(), calls=%async_computation.5 | async-start | bytes 4718592 | tf_op jit(solution)/shard_map/all_gather | solution.py:44
  12.2 91.8 %reduce-scatter.2.cloned.1.call-start = ((), (), s32[]{:S(2)}) async-start(), calls=%async_computation.2 | async-start | bytes 786432 | tf_op jit(solution)/shard_map/reduce_scatter | solution.py:19
  20.8 83.1 %copy-start.1 = (f32[1,2,512,128]{3,2,1,0:T(8,128)S(1)}, f32[1,2,512,128]{3,2,1,0:T(8,128)}, u32[]{:S(2)}) copy-start(f32[1,2,512,128]{3,2,1,0:T(8,128)} %param.4) | copy-start | bytes 1572868
  97.3 41.4 %all-reduce.6.cloned.1.call-start = ((), (), s32[]{:S(2)}) async-start(), calls=%async_computation.3 | async-start | bytes 1048576 | tf_op jit(solution)/shard_map/psum | solution.py:32
  108.7 74.3 %all-reduce.8.cloned.1.call-start = ((), (), s32[]{:S(2)}) async-start(), calls=%async_computation.4 | async-start | bytes 1048576 | tf_op jit(solution)/shard_map/psum | solution.py:78
  144.3 38.8 %copy-start = (f32[1024,128]{1,0:T(8,128)S(1)}, f32[1024,128]{1,0:T(8,128)}, u32[]{:S(2)}) copy-start(f32[1024,128]{1,0:T(8,128)} %all-reduce.4.cloned.1.call-done) | copy-start | bytes 1572868
Sparse Core Ops, SparseCore 0:
  11.7 31.3 all-reduce.3
  97.4 6.5 reduce-scatter.1
  108.9 29.7 all-reduce.5
  154.4 28.6 all-reduce.7
Sparse Core Ops, SparseCore 1:
  14.2 75.2 all-gather.3
where the time goes:
time: 195 us; the launch traced here: 194 us
  waiting for transfers between devices  135 us (69%)
  matrix products  33 us (17%)
  between operations  14.6 us (7%)
  local copies, waits for them, and re-layouts  8.97 us (5%)
  blocking collectives  2.36 us (1%)
    psum x2, waiting for transfers between devices, invert_level(): return lax.psum(inverse_term, 'rows')  52.1 us
    all_gather x1, waiting for transfers between devices, per_device(): front_factor = lax.all_gather(factor[0], 'shots', axis=1, tiled=True)  46.4 us
    psum x1, waiting for transfers between devices, per_device(): own_columns = lax.psum(transposed, 'rows')  28.8 us
    dot_general x1, matrix products, per_device(): jnp.einsum('grs,grn->sn', factor_tiles, collected[1], precision=highest,...  9.96 us
    dot_general x2, matrix products, invert_level(): jnp.dot(inverse_block, own_rows, precision=lax.Precision.HIGHEST, preferr...  8.97 us
    dot_general x1, matrix products, per_device(): jnp.einsum('lgrs,lsn->grn', factor_tiles, lower_solved, precision=highest...  7.7 us
    reduce_scatter x1, waiting for transfers between devices, group_reduce(): lax.psum_scatter(partial_value, 'depth', scatter_dimension=0, tiled=True)  6.63 us
    dot_general x2, matrix products, per_device(): lax.dot_general(inverse_diagonal[0, tier_index], target, (((0,), (0,)), (...  6.22 us
  transfers between devices with their start and end apart: 5, of which 5 were waited for; matrix products, arithmetic and copies ran while one was open for 4% of the time, Pallas kernels for 0%

commit v1 on v0

--- a/solution.py
+++ b/solution.py
@@ -75,7 +75,7 @@
                 precision=highest,
                 preferred_element_type=jnp.float32,
             )
-            own_columns = lax.psum(transposed, "rows")
+            own_columns = jnp.sum(lax.all_gather(transposed, "rows"), axis=0)
             target = target - own_columns
         answer = lax.dot_general(
             inverse_diagonal[0, tier_index],

time: 195 us -> 189 us (0.969)
  waiting for transfers between devices: 135 us -> 127 us
    psum x1 -> x0, waiting for transfers between devices: 28.8 us -> none  [per_device(): own_columns = lax.psum(transposed, 'rows')]
    all_gather x0 -> x1, waiting for transfers between devices: none -> 21.4 us  [per_device(): own_columns = jnp.sum(lax.all_gather(transposed, 'rows'), axis=0)]
  transfers between devices with their start and end apart: 5 -> 5, of which waited for: 5 -> 5; matrix products, arithmetic and copies ran while one was open for 4% -> 5% of each run, Pallas kernels for 0% -> 0%
where the time goes in v1:
time: 189 us; the launch traced here: 188 us
  waiting for transfers between devices  127 us (67%)
  matrix products  32.8 us (17%)
  between operations  14.6 us (8%)
  local copies, waits for them, and re-layouts  8.97 us (5%)
  blocking collectives  2.36 us (1%)
  other arithmetic  2.09 us (1%)
    psum x2, waiting for transfers between devices, invert_level(): return lax.psum(inverse_term, 'rows')  52.1 us
    all_gather x1, waiting for transfers between devices, per_device(): front_factor = lax.all_gather(factor[0], 'shots', axis=1, tiled=True)  46.4 us
    all_gather x1, waiting for transfers between devices, per_device(): own_columns = jnp.sum(lax.all_gather(transposed, 'rows'), axis=0)  21.4 us
    dot_general x1, matrix products, per_device(): jnp.einsum('grs,grn->sn', factor_tiles, collected[1], precision=highest,...  9.96 us
    dot_general x2, matrix products, invert_level(): jnp.dot(inverse_block, own_rows, precision=lax.Precision.HIGHEST, preferr...  8.97 us
    dot_general x1, matrix products, per_device(): jnp.einsum('lgrs,lsn->grn', factor_tiles, lower_solved, precision=highest...  7.7 us
    reduce_scatter x1, waiting for transfers between devices, group_reduce(): lax.psum_scatter(partial_value, 'depth', scatter_dimension=0, tiled=True)  6.63 us
    dot_general x2, matrix products, per_device(): lax.dot_general(inverse_diagonal[0, tier_index], target, (((0,), (0,)), (...  6.04 us
  transfers between devices with their start and end apart: 5, of which 5 were waited for; matrix products, arithmetic and copies ran while one was open for 5% of the time, Pallas kernels for 0%

profile of v1, /device:TPU:0, one launch (start us, length us, event | category | flops | bytes accessed | tf_op | source)
XLA Modules:
  0.0 188.2 jit_solution(5667522238775290834)
XLA Ops:
  7.4 0.0 all-reduce.3.cloned.1.call-start
  7.4 4.2 %fusion.6 = f32[1024,128]{1,0:T(8,128)} fusion(f32[1,2,1024,512]{3,2,1,0:T(8,128)} %param.7, f32[1,2,512,128]{3,2,1,0:T(8,128)} %param.4), kind=kOutput, calls=%fused_computation.7 | convolution fusion | flops 805306368 | bytes 2883584 | tf_op jit(solution)/shard_map/dot_general | solution.py:29
  11.5 0.0 all-reduce.3.cloned.1.call-update
  11.6 0.0 all-gather.6.cloned.1.call-start
  11.6 0.5 all-gather.6.cloned.1.call-update
  12.2 0.0 reduce-scatter.2.cloned.1.call-start
  12.2 0.7 convert_bitcast_fusion
  12.9 0.1 copy.5
  13.0 0.1 convolution_bitcast_fusion
  13.1 0.2 copy.6
  13.3 2.6 %broadcast_in_dim.11 = f32[2,512,8,128]{3,2,1,0:T(8,128)} broadcast(f32[2,512,8]{2,1,0:T(8,128)S(1)} %copy.6), dimensions={0,1,2} | broadcast | bytes 4227072 | tf_op jit(solution)/shard_map/broadcast_in_dim | solution.py:15
  15.9 4.9 %reshape.30 = f32[2,512,1024]{2,1,0:T(8,128)} reshape(f32[2,512,8,128]{3,2,1,0:T(8,128)} %broadcast_in_dim.11) | data formatting | bytes 8388608 | tf_op jit(solution)/shard_map/reshape | solution.py:15
  20.8 22.3 %all-reduce.3.cloned.1.call-done = f32[1024,128]{1,0:T(8,128)} async-done(((f32[1024,128]{1,0:T(8,128)}), f32[1024,128]{1,0:T(8,128)}) %all-reduce.3.cloned.1.call-update) | async-done | bytes 524304 | tf_op jit(solution)/shard_map/psum | solution.py:32
  43.1 46.4 %all-gather.6.cloned.1.call-done = f32[1,2,512,1024]{3,2,1,0:T(8,128)} async-done(((f32[1,2,64,1024]{3,2,1,0:T(8,128)}), f32[1,2,512,1024]{3,2,1,0:T(8,128)}) %all-gather.6.cloned.1.call-update) | async-done | bytes 4194320 | tf_op jit(solution)/shard_map/all_gather | solution.py:44
  89.5 7.7 %fusion.13 = f32[2,512,128]{2,1,0:T(8,128)} fusion(f32[2,512,1024]{2,1,0:T(8,128)} %reshape.30, f32[1,2,512,1024]{3,2,1,0:T(8,128)} %all-gather.6.cloned.1.call-done, f32[1024,128]{1,0:T(8,128)} %all-reduce.3.cloned.1.call-done), kind=kOutput, calls=%fused_computation.14 | convolution fusion | flops 1611661312 | bytes 9437184 | tf_op jit(solution)/shard_map/lgrs,lsn->grn/dot_general | solution.py:54
  97.2 0.0 reduce-scatter.2.cloned.1.call-update
  97.3 0.0 all-reduce.5.cloned.1.call-start
  97.3 6.6 %reduce-scatter.2.cloned.1.call-done = f32[1,512,128]{2,1,0:T(8,128)} async-done(((f32[2,512,128]{2,1,0:T(8,128)}), f32[1,512,128]{2,1,0:T(8,128)}) %reduce-scatter.2.cloned.1.call-update) | async-done | bytes 262160 | tf_op jit(solution)/shard_map/reduce_scatter | solution.py:19
  103.9 4.8 %fusion.15 = f32[1024,128]{0,1:T(8,128)} fusion(f32[1,2,1024,512]{3,2,1,0:T(8,128)} %param.7, f32[1,512,128]{2,1,0:T(8,128)} %reduce-scatter.2.cloned.1.call-done, f32[1,2,512,128]{3,2,1,0:T(8,128)S(1)} %copy-done.1), kind=kOutput, calls=%fused_computation.16 | convolution fusion | flops 805371904 | bytes 3145728 | tf_op jit(solution)/shard_map/dot_general | solution.py:29
  108.7 0.0 all-reduce.5.cloned.1.call-update
  108.7 0.0 all-gather.8.cloned.1.call-start
  108.8 29.9 %all-reduce.5.cloned.1.call-done = f32[1024,128]{0,1:T(8,128)} async-done(((f32[1024,128]{0,1:T(8,128)}), f32[1024,128]{0,1:T(8,128)}) %all-reduce.5.cloned.1.call-update) | async-done | bytes 524304 | tf_op jit(solution)/shard_map/psum | solution.py:32
  138.7 3.1 %fusion = f32[128,512]{1,0:T(8,128)S(1)} fusion(f32[1024,128]{0,1:T(8,128)} %all-reduce.5.cloned.1.call-done, f32[1,2,1024,512]{3,2,1,0:T(8,128)} %param.7), kind=kOutput, calls=%fused_computation.1 | convolution fusion | flops 805306368 | bytes 2883584 | tf_op jit(solution)/shard_map/dot_general | solution.py:80
  141.7 2.4 %all-gather.1 = f32[1024,128]{0,1:T(8,128)S(1)} all-gather(f32[512,128]{0,1:T(8,128)S(1)} %bitcast.64), channel_id=3, replica_groups=mesh['depth'=2,'rows'=2,'shots'=8] {'depth'}, dimensions={0}, use_global_device_ids=true | all-gather | bytes 786432 | tf_op jit(solution)/shard_map/all_gather | solution.py:24
  144.1 0.2 copy.11
  144.3 10.0 %fusion.14 = f32[1024,128]{1,0:T(8,128)} fusion(f32[2,512,128]{2,1,0:T(8,128)S(1)} %bitcast.66, f32[2,512,1024]{2,1,0:T(8,128)} %reshape.30, f32[1,2,512,1024]{3,2,1,0:T(8,128)} %all-gather.6.cloned.1.call-done), kind=kOutput, calls=%fused_computation.15 | convolution fusion | flops 1611661312 | bytes 9437184 | tf_op jit(solution)/shard_map/grs,grn->sn/dot_general | solution.py:71
  154.3 0.0 all-gather.8.cloned.1.call-update
  154.3 21.4 %all-gather.8.cloned.1.call-done = f32[2048,128]{1,0:T(8,128)} async-done(((f32[1024,128]{1,0:T(8,128)}), f32[2048,128]{1,0:T(8,128)}) %all-gather.8.cloned.1.call-update) | async-done | bytes 1048592 | tf_op jit(solution)/shard_map/all_gather | solution.py:78
  175.7 1.3 reduce_sum.9
  177.1 0.0 copy-done
  177.1 3.0 %fusion.18 = f32[1,512,128]{1,2,0:T(8,128)S(1)} fusion(f32[1,2,1024,512]{3,2,1,0:T(8,128)} %param.7, f32[1024,128]{1,0:T(8,128)S(1)} %copy-done, f32[1024,128]{1,0:T(8,128)S(1)} %reduce_sum.9), kind=kOutput, calls=%fused_computation.17 | convolution fusion | flops 805437440 | bytes 3407872 | tf_op jit(solution)/shard_map/dot_general | solution.py:80
  180.1 1.0 copy.9
  (5 shorter events, 0.1 us)
Async XLA Ops:
  7.4 35.7 %all-reduce.3.cloned.1.call-start = ((), (), s32[]{:S(2)}) async-start(), calls=%async_computation.1 | async-start | bytes 1048576 | tf_op jit(solution)/shard_map/psum | solution.py:32
  11.6 78.0 %all-gather.6.cloned.1.call-start = ((), (), s32[]{:S(2)}) async-start(), calls=%async_computation.4 | async-start | bytes 4718592 | tf_op jit(solution)/shard_map/all_gather | solution.py:44
  12.2 91.8 %reduce-scatter.2.cloned.1.call-start = ((), (), s32[]{:S(2)}) async-start(), calls=%async_computation.2 | async-start | bytes 786432 | tf_op jit(solution)/shard_map/reduce_scatter | solution.py:19
  20.8 83.1 %copy-start.1 = (f32[1,2,512,128]{3,2,1,0:T(8,128)S(1)}, f32[1,2,512,128]{3,2,1,0:T(8,128)}, u32[]{:S(2)}) copy-start(f32[1,2,512,128]{3,2,1,0:T(8,128)} %param.4) | copy-start | bytes 1572868
  97.3 41.4 %all-reduce.5.cloned.1.call-start = ((), (), s32[]{:S(2)}) async-start(), calls=%async_computation.3 | async-start | bytes 1048576 | tf_op jit(solution)/shard_map/psum | solution.py:32
  108.7 67.0 %all-gather.8.cloned.1.call-start = ((), (), s32[]{:S(2)}) async-start(), calls=%async_computation.5 | async-start | bytes 1572864 | tf_op jit(solution)/shard_map/all_gather | solution.py:78
  144.3 32.8 %copy-start = (f32[1024,128]{1,0:T(8,128)S(1)}, f32[1024,128]{1,0:T(8,128)}, u32[]{:S(2)}) copy-start(f32[1024,128]{1,0:T(8,128)} %all-reduce.3.cloned.1.call-done) | copy-start | bytes 1572868
Sparse Core Ops, SparseCore 0:
  11.7 31.3 all-reduce.2
  97.4 6.5 reduce-scatter.1
  108.9 29.7 all-reduce.4
  154.4 21.2 all-gather.7
Sparse Core Ops, SparseCore 1:
  14.2 75.2 all-gather.5
